TPU v7x, 256 devices: a whole 4x4x8 slice. The times are simulated.
256 devices in a mesh: row: 32 (over x_hi, z, core), col: 8 (over y, x_lo).
Axes of the slice: x: 4 (x_hi: 2, x_lo: 2; x = x_hi * 2 + x_lo), y: 4, z: 8, core: 2. Of those that a mesh axis runs over, the one named last changes fastest.
Arguments:
- x_tiles: bfloat16 [64, 32, 1, 128, 128], P('row', 'col'), may hold values from -0.5390625 to 0.5390625
- x_cols: int32 [64, 32, 1], P('row', 'col'), may hold values from 0 to 1, as said below
- keep_cols: int32 [64, 32, 2], P('row', 'col'), may hold values from 0 to 1, as said below
Outputs:
- square: bfloat16 [64, 32, 2, 128, 128], P('row', 'col')
- purified: bfloat16 [64, 32, 2, 128, 128], P('row', 'col')
Inputs may be any that keep to these rules, and one draw needn't show every extreme that they name: `x_cols`: within each block row and column panel the 1 entries are distinct. `keep_cols`: within each block row and column panel the 2 entries are distinct.
All inputs are finite; a program needn't handle non-finite values.
Results may differ from a plain program's by a relative error of at most 0.0049.
Values may be sent and summed in bfloat16 or wider, within the bound.
A program may use at most 64 MiB of HBM per device.

v0:
```python
import jax
import jax.numpy as jnp
from jax import lax
from jax.sharding import PartitionSpec as P


def shifted(value, axis, steps):
    count = lax.axis_size(axis)
    pairs = [(source, (source + steps) % count) for source in range(count)]
    return lax.ppermute(value, axis, pairs)


def collect(local):
    groups = lax.axis_size("col")
    collected = [local] * groups
    current = local
    for step in range(1, groups):
        current = shifted((current[0], current[1]), "col", 1)
        collected[step] = current
    stack_tiles = jnp.stack([entry[0] for entry in collected], axis=0)
    stack_cols = jnp.stack([entry[1] for entry in collected], axis=0)
    return (stack_tiles, stack_cols)


def add_slabs(a_stack, kept_cols, carry, piece, start):
    stack_tiles, stack_cols = a_stack
    piece_tiles, piece_cols = piece
    groups = stack_tiles.shape[0]
    slab_rows = stack_tiles.shape[1]
    group_panels = stack_tiles.shape[2]
    my_group = lax.axis_index("col")
    count = piece_tiles.shape[0] // slab_rows

    def one_slab(step, total):
        slab_idx = start // slab_rows + step
        owner = slab_idx // group_panels
        panel_in = slab_idx % group_panels
        slot = (my_group - owner) % groups
        a_tiles = lax.dynamic_index_in_dim(
            lax.dynamic_index_in_dim(stack_tiles, slot, 0, False), panel_in, 1, False
        )
        a_cols = lax.dynamic_index_in_dim(
            lax.dynamic_index_in_dim(stack_cols, slot, 0, False), panel_in, 1, False
        )
        b_tiles = lax.dynamic_slice_in_dim(piece_tiles, step * slab_rows, slab_rows, 0)
        b_cols = lax.dynamic_slice_in_dim(piece_cols, step * slab_rows, slab_rows, 0)
        b_rows = jnp.take(b_tiles, a_cols, axis=0)
        b_ids = jnp.take(b_cols, a_cols, axis=0)
        matched = (b_ids[:, :, :, None, :] == kept_cols[:, None, :, :, None]).astype(jnp.bfloat16)
        selected = jnp.einsum(
            "iaqtb,iaqbnk->iaqtnk", matched, b_rows, preferred_element_type=jnp.float32
        ).astype(jnp.bfloat16)
        return total + jnp.einsum(
            "iamn,iaqtnk->iqtmk", a_tiles, selected, preferred_element_type=jnp.float32
        )

    return lax.fori_loop(0, count, one_slab, carry)


def shards(x_tiles, x_cols, keep_cols):
    tile_size = x_tiles.shape[-1]
    initial = jnp.zeros(
        (x_tiles.shape[0], x_tiles.shape[1], keep_cols.shape[2], tile_size, tile_size), jnp.float32
    )
    whole = (
        lax.all_gather(x_tiles, "row", axis=0, tiled=True),
        lax.all_gather(x_cols, "row", axis=0, tiled=True),
    )

    def through(a_stack):
        return add_slabs(a_stack, keep_cols, initial, whole, 0)

    square = through(collect((x_tiles, x_cols))).astype(jnp.bfloat16)
    cube = through(collect((square, keep_cols)))
    purified = (3.0 * square.astype(jnp.float32) - 2.0 * cube).astype(jnp.bfloat16)
    return (square, purified)


def solution(mesh):
    in_specs = (P("row", "col", None, None, None), P("row", "col", None), P("row", "col", None))
    out_specs = (P("row", "col", None, None, None), P("row", "col", None, None, None))
    return jax.shard_map(shards, mesh=mesh, in_specs=in_specs, out_specs=out_specs, check_vma=False)
```

profile of v0, /device:TPU:68, one launch (start us, length us, event | category | flops | bytes accessed | tf_op | source)
XLA Modules:
  0.0 549.6 jit_solution(11523895976069203512)
XLA Ops:
  10.1 1.8 collective-permute-start
  12.0 7.1 %collective-permute-done.7 = bf16[2,4,1,128,128]{4,3,0,1,2:T(8,128)(2,1)S(1)} collective-permute-done((bf16[2,4,1,128,128]{4,3,0,1,2:T(8,128)(2,1)S(1)}, bf16[2,4,1,128,128]{4,3,0,1,2:T(8,128)(2,1)S(1)}, u32[]{:S(2)}, u32[]{:S(2)}) %collective-permute-start.7) | collective-permute-done | bytes 262176 | tf_op jit(solution)/shard_map/ppermute | solution.py:10
  21.6 37.1 %all_gather.6 = s32[64,4,1]{1,2,0:T(1,128)S(1)} all-gather(s32[2,4,1]{1,2,0:T(1,128)} %param.8), channel_id=1, replica_groups=mesh['row'=32,'col'=8] {'row'}, dimensions={0}, use_global_device_ids=true | all-gather | bytes 1056 | tf_op jit(solution)/shard_map/all_gather | solution.py:67
  59.4 2.3 collective-permute-start.1
  61.8 3.8 collective-permute-done.1
  65.7 12.1 %collective-permute-done.2 = s32[2,4,1]{1,2,0:T(1,128)S(1)} collective-permute-done((s32[2,4,1]{1,2,0:T(1,128)S(1)}, s32[2,4,1]{1,2,0:T(1,128)S(1)}, u32[]{:S(2)}, u32[]{:S(2)}) %collective-permute-start.2) | collective-permute-done | bytes 64 | tf_op jit(solution)/shard_map/ppermute | solution.py:10
  77.8 5.8 %collective-permute-done.3 = s32[2,4,1]{1,2,0:T(1,128)S(1)} collective-permute-done((s32[2,4,1]{1,2,0:T(1,128)S(1)}, s32[2,4,1]{1,2,0:T(1,128)S(1)}, u32[]{:S(2)}, u32[]{:S(2)}) %collective-permute-start.3) | collective-permute-done | bytes 64 | tf_op jit(solution)/shard_map/ppermute | solution.py:10
  84.7 4.6 collective-permute-done.4
  89.3 9.8 %collective-permute-done.5 = s32[2,4,1]{1,2,0:T(1,128)S(1)} collective-permute-done((s32[2,4,1]{1,2,0:T(1,128)S(1)}, s32[2,4,1]{1,2,0:T(1,128)S(1)}, u32[]{:S(2)}, u32[]{:S(2)}) %collective-permute-start.5) | collective-permute-done | bytes 64 | tf_op jit(solution)/shard_map/ppermute | solution.py:10
  99.1 5.7 %collective-permute-done.6 = s32[2,4,1]{1,2,0:T(1,128)S(1)} collective-permute-done((s32[2,4,1]{1,2,0:T(1,128)S(1)}, s32[2,4,1]{1,2,0:T(1,128)S(1)}, u32[]{:S(2)}, u32[]{:S(2)}) %collective-permute-start.6) | collective-permute-done | bytes 64 | tf_op jit(solution)/shard_map/ppermute | solution.py:10
  106.5 9.1 %collective-permute-done.11 = bf16[2,4,1,128,128]{4,3,0,1,2:T(8,128)(2,1)S(1)} collective-permute-done((bf16[2,4,1,128,128]{4,3,0,1,2:T(8,128)(2,1)S(1)}, bf16[2,4,1,128,128]{4,3,0,1,2:T(8,128)(2,1)S(1)}, u32[]{:S(2)}, u32[]{:S(2)}) %collective-permute-start.11) | collective-permute-done | bytes 262176 | tf_op jit(solution)/shard_map/ppermute | solution.py:10
  117.0 9.5 %collective-permute-done.12 = bf16[2,4,1,128,128]{4,3,0,1,2:T(8,128)(2,1)S(1)} collective-permute-done((bf16[2,4,1,128,128]{4,3,0,1,2:T(8,128)(2,1)S(1)}, bf16[2,4,1,128,128]{4,3,0,1,2:T(8,128)(2,1)S(1)}, u32[]{:S(2)}, u32[]{:S(2)}) %collective-permute-start.12) | collective-permute-done | bytes 262176 | tf_op jit(solution)/shard_map/ppermute | solution.py:10
  127.9 7.0 %collective-permute-done.13 = bf16[2,4,1,128,128]{4,3,0,1,2:T(8,128)(2,1)S(1)} collective-permute-done((bf16[2,4,1,128,128]{4,3,0,1,2:T(8,128)(2,1)S(1)}, bf16[2,4,1,128,128]{4,3,0,1,2:T(8,128)(2,1)S(1)}, u32[]{:S(2)}, u32[]{:S(2)}) %collective-permute-start.13) | collective-permute-done | bytes 262176 | tf_op jit(solution)/shard_map/ppermute | solution.py:10
  135.6 134.6 %while.34 = (s32[]{:T(128)}, f32[2,4,2,128,128]{3,4,2,1,0:T(8,128)S(1)}, s32[]{:T(128)}, s32[8,2,4,1]{1,3,2,0:T(1,128)S(1)}, s32[64,4,1]{1,0,2:T(8,128)S(1)}, /*...) while((s32[]{:T(128)}, ...), condition=%wide.region_1.2_spmd.clone, body=%wide.region_0.1_spmd.clone.sunk | while | flops 68420704 | bytes 5575707 | solution.py:57
  270.7 16.5 %collective-permute-done.21 = bf16[2,4,2,128,128]{4,3,2,1,0:T(8,128)(2,1)S(1)} collective-permute-done((bf16[2,4,2,128,128]{4,3,2,1,0:T(8,128)(2,1)S(1)}, bf16[2,4,2,128,128]{4,3,2,1,0:T(8,128)(2,1)S(1)}, u32[]{:S(2)}, u32[]{:S(2)}) %collective-permute-start.21) | collective-permute-done | bytes 524320 | tf_op jit(solution)/shard_map/ppermute | solution.py:10
  287.2 16.2 %collective-permute-done.22 = bf16[2,4,2,128,128]{4,3,2,1,0:T(8,128)(2,1)S(1)} collective-permute-done((bf16[2,4,2,128,128]{4,3,2,1,0:T(8,128)(2,1)S(1)}, bf16[2,4,2,128,128]{4,3,2,1,0:T(8,128)(2,1)S(1)}, u32[]{:S(2)}, u32[]{:S(2)}) %collective-permute-start.22) | collective-permute-done | bytes 524320 | tf_op jit(solution)/shard_map/ppermute | solution.py:10
  303.5 13.9 %collective-permute-done.15 = s32[2,4,2]{1,2,0:T(2,128)S(1)} collective-permute-done((s32[2,4,2]{1,2,0:T(2,128)S(1)}, s32[2,4,2]{1,2,0:T(2,128)S(1)}, u32[]{:S(2)}, u32[]{:S(2)}) %collective-permute-start.15) | collective-permute-done | bytes 96 | tf_op jit(solution)/shard_map/ppermute | solution.py:10
  317.3 5.7 %collective-permute-done.16 = s32[2,4,2]{1,2,0:T(2,128)S(1)} collective-permute-done((s32[2,4,2]{1,2,0:T(2,128)S(1)}, s32[2,4,2]{1,2,0:T(2,128)S(1)}, u32[]{:S(2)}, u32[]{:S(2)}) %collective-permute-start.16) | collective-permute-done | bytes 96 | tf_op jit(solution)/shard_map/ppermute | solution.py:10
  323.0 5.7 %collective-permute-done.17 = s32[2,4,2]{1,2,0:T(2,128)S(1)} collective-permute-done((s32[2,4,2]{1,2,0:T(2,128)S(1)}, s32[2,4,2]{1,2,0:T(2,128)S(1)}, u32[]{:S(2)}, u32[]{:S(2)}) %collective-permute-start.17) | collective-permute-done | bytes 96 | tf_op jit(solution)/shard_map/ppermute | solution.py:10
  328.7 10.4 %collective-permute-done.18 = s32[2,4,2]{1,2,0:T(2,128)S(1)} collective-permute-done((s32[2,4,2]{1,2,0:T(2,128)S(1)}, s32[2,4,2]{1,2,0:T(2,128)S(1)}, u32[]{:S(2)}, u32[]{:S(2)}) %collective-permute-start.18) | collective-permute-done | bytes 96 | tf_op jit(solution)/shard_map/ppermute | solution.py:10
  339.1 5.7 %collective-permute-done.19 = s32[2,4,2]{1,2,0:T(2,128)S(1)} collective-permute-done((s32[2,4,2]{1,2,0:T(2,128)S(1)}, s32[2,4,2]{1,2,0:T(2,128)S(1)}, u32[]{:S(2)}, u32[]{:S(2)}) %collective-permute-start.19) | collective-permute-done | bytes 96 | tf_op jit(solution)/shard_map/ppermute | solution.py:10
  344.8 5.7 %collective-permute-done.20 = s32[2,4,2]{1,2,0:T(2,128)S(1)} collective-permute-done((s32[2,4,2]{1,2,0:T(2,128)S(1)}, s32[2,4,2]{1,2,0:T(2,128)S(1)}, u32[]{:S(2)}, u32[]{:S(2)}) %collective-permute-start.20) | collective-permute-done | bytes 96 | tf_op jit(solution)/shard_map/ppermute | solution.py:10
  350.8 7.0 %collective-permute-done.25 = bf16[2,4,2,128,128]{4,3,2,1,0:T(8,128)(2,1)} collective-permute-done((bf16[2,4,2,128,128]{4,3,2,1,0:T(8,128)(2,1)}, bf16[2,4,2,128,128]{4,3,2,1,0:T(8,128)(2,1)}, u32[]{:S(2)}, u32[]{:S(2)}) %collective-permute-start.25) | collective-permute-done | bytes 524320 | tf_op jit(solution)/shard_map/ppermute | solution.py:10
  358.0 13.3 %collective-permute-done.26 = bf16[2,4,2,128,128]{4,3,2,1,0:T(8,128)(2,1)S(1)} collective-permute-done((bf16[2,4,2,128,128]{4,3,2,1,0:T(8,128)(2,1)}, bf16[2,4,2,128,128]{4,3,2,1,0:T(8,128)(2,1)S(1)}, u32[]{:S(2)}, u32[]{:S(2)}) %collective-permute-start.26) | collective-permute-done | bytes 524320 | tf_op jit(solution)/shard_map/ppermute | solution.py:10
  373.7 8.9 %collective-permute-done.27 = bf16[2,4,2,128,128]{4,3,2,1,0:T(8,128)(2,1)S(1)} collective-permute-done((bf16[2,4,2,128,128]{4,3,2,1,0:T(8,128)(2,1)S(1)}, bf16[2,4,2,128,128]{4,3,2,1,0:T(8,128)(2,1)S(1)}, u32[]{:S(2)}, u32[]{:S(2)}) %collective-permute-start.27) | collective-permute-done | bytes 524320 | tf_op jit(solution)/shard_map/ppermute | solution.py:10
  382.7 2.0 copy-done.1
  384.7 155.7 %while.35 = (s32[]{:T(128)}, f32[2,4,2,128,128]{3,4,2,1,0:T(8,128)S(1)}, s32[]{:T(128)}, s32[8,2,4,2]{3,1,2,0:T(2,128)S(1)}, s32[64,4,1]{1,0,2:T(8,128)S(1)}, /*...) while((s32[]{:T(128)}, ...), condition=%wide.region_3.4_spmd.clone, body=%wide.region_2.3_spmd.clone.sunk | while | flops 136316064 | bytes 8525329 | solution.py:57
  387.8 1.7 fusion.22
  392.6 1.7 fusion.22
  397.5 1.7 fusion.22
  402.4 1.7 fusion.22
  407.2 1.7 fusion.22
  412.1 1.7 fusion.22
  421.8 1.7 fusion.22
  426.7 1.7 fusion.22
  431.6 1.7 fusion.22
  436.4 1.7 fusion.22
  446.2 1.7 fusion.22
  451.0 1.7 fusion.22
  455.9 1.7 fusion.22
  460.8 1.7 fusion.22
  470.5 1.7 fusion.22
  480.2 1.7 fusion.22
  485.1 1.7 fusion.22
  490.0 1.7 fusion.22
  494.9 1.7 fusion.22
  504.6 1.7 fusion.22
  540.7 2.0 subtract_convert_fusion
  (893 shorter events, 264.8 us)
Async XLA Ops:
  7.2 128.5 %all-gather.2.cloned.1.call-start = ((), (), s32[]{:S(2)}) async-start(), calls=%async_computation | async-start | bytes 8650752 | tf_op jit(solution)/shard_map/all_gather | solution.py:66
  8.9 10.2 %collective-permute-start.7 = (bf16[2,4,1,128,128]{4,3,0,1,2:T(8,128)(2,1)S(1)}, bf16[2,4,1,128,128]{4,3,0,1,2:T(8,128)(2,1)S(1)}, u32[]{:S(2)}, u32[]{:S(2)}) collective-permute-start(bf16[2,4,1,128,128]{4,3,0,1,2:T(8,128)(2,1)S(1)} %copy.45), channel_id=1, source_target_pairs={{0,1},{1,2},{2,3},{3,4},{4,5},{5,6},{6,7},{7,0},{8,9},{9,10},{10,1... | collective-permute-start | bytes 786440 | tf_op jit(solution)/shard_map/ppermute | solution.py:10
  10.1 49.3 %collective-permute-start = (s32[2,4,1]{1,2,0:T(1,128)}, s32[2,4,1]{1,2,0:T(1,128)S(1)}, u32[]{:S(2)}, u32[]{:S(2)}) collective-permute-start(s32[2,4,1]{1,2,0:T(1,128)} %param.8), channel_id=1, source_target_pairs={{0,1},{1,2},{2,3},{3,4},{4,5},{5,6},{6,7},{7,0},{8,9},{9,10},{10,1... | collective-permute-start | bytes 104 | tf_op jit(solution)/shard_map/ppermute | solution.py:10
  19.1 42.6 %collective-permute-start.8 = (bf16[2,4,1,128,128]{4,3,0,1,2:T(8,128)(2,1)S(1)}, bf16[2,4,1,128,128]{4,3,0,1,2:T(8,128)(2,1)S(1)}, u32[]{:S(2)}, u32[]{:S(2)}) collective-permute-start(bf16[2,4,1,128,128]{4,3,0,1,2:T(8,128)(2,1)S(1)} %collective-permute-done.7), channel_id=1, source_target_pairs={{0,1},{1,2},{2,3},{3,4},{4,5},{5,6},{6,7},{7,0},{8,9},{9,10},{10,1... | collective-permute-start | bytes 786440 | tf_op jit(solution)/shard_map/ppermute | solution.py:10
  59.4 6.3 %collective-permute-start.1 = (s32[2,4,1]{1,2,0:T(1,128)S(1)}, s32[2,4,1]{1,2,0:T(1,128)S(1)}, u32[]{:S(2)}, u32[]{:S(2)}) collective-permute-start(s32[2,4,1]{1,2,0:T(1,128)S(1)} %collective-permute-done), channel_id=1, source_target_pairs={{0,1},{1,2},{2,3},{3,4},{4,5},{5,6},{6,7},{7,0},{8,9},{9,10},{10,1... | collective-permute-start | bytes 104 | tf_op jit(solution)/shard_map/ppermute | solution.py:10
  61.8 21.8 %collective-permute-start.9 = (bf16[2,4,1,128,128]{4,3,0,1,2:T(8,128)(2,1)S(1)}, bf16[2,4,1,128,128]{4,3,0,1,2:T(8,128)(2,1)S(1)}, u32[]{:S(2)}, u32[]{:S(2)}) collective-permute-start(bf16[2,4,1,128,128]{4,3,0,1,2:T(8,128)(2,1)S(1)} %collective-permute-done.8), channel_id=1, source_target_pairs={{0,1},{1,2},{2,3},{3,4},{4,5},{5,6},{6,7},{7,0},{8,9},{9,10},{10,1... | collective-permute-start | bytes 786440 | tf_op jit(solution)/shard_map/ppermute | solution.py:10
  65.7 12.1 %collective-permute-start.2 = (s32[2,4,1]{1,2,0:T(1,128)S(1)}, s32[2,4,1]{1,2,0:T(1,128)S(1)}, u32[]{:S(2)}, u32[]{:S(2)}) collective-permute-start(s32[2,4,1]{1,2,0:T(1,128)S(1)} %collective-permute-done.1), channel_id=1, source_target_pairs={{0,1},{1,2},{2,3},{3,4},{4,5},{5,6},{6,7},{7,0},{8,9},{9,10},{10,1... | collective-permute-start | bytes 104 | tf_op jit(solution)/shard_map/ppermute | solution.py:10
  77.8 5.8 %collective-permute-start.3 = (s32[2,4,1]{1,2,0:T(1,128)S(1)}, s32[2,4,1]{1,2,0:T(1,128)S(1)}, u32[]{:S(2)}, u32[]{:S(2)}) collective-permute-start(s32[2,4,1]{1,2,0:T(1,128)S(1)} %collective-permute-done.2), channel_id=1, source_target_pairs={{0,1},{1,2},{2,3},{3,4},{4,5},{5,6},{6,7},{7,0},{8,9},{9,10},{10,1... | collective-permute-start | bytes 104 | tf_op jit(solution)/shard_map/ppermute | solution.py:10
  83.6 5.7 %collective-permute-start.4 = (s32[2,4,1]{1,2,0:T(1,128)S(1)}, s32[2,4,1]{1,2,0:T(1,128)S(1)}, u32[]{:S(2)}, u32[]{:S(2)}) collective-permute-start(s32[2,4,1]{1,2,0:T(1,128)S(1)} %collective-permute-done.3), channel_id=1, source_target_pairs={{0,1},{1,2},{2,3},{3,4},{4,5},{5,6},{6,7},{7,0},{8,9},{9,10},{10,1... | collective-permute-start | bytes 104 | tf_op jit(solution)/shard_map/ppermute | solution.py:10
  83.6 21.3 %collective-permute-start.10 = (bf16[2,4,1,128,128]{4,3,0,1,2:T(8,128)(2,1)S(1)}, bf16[2,4,1,128,128]{4,3,0,1,2:T(8,128)(2,1)S(1)}, u32[]{:S(2)}, u32[]{:S(2)}) collective-permute-start(bf16[2,4,1,128,128]{4,3,0,1,2:T(8,128)(2,1)S(1)} %collective-permute-done.9), channel_id=1, source_target_pairs={{0,1},{1,2},{2,3},{3,4},{4,5},{5,6},{6,7},{7,0},{8,9},{9,10},{10,1... | collective-permute-start | bytes 786440 | tf_op jit(solution)/shard_map/ppermute | solution.py:10
  89.3 9.8 %collective-permute-start.5 = (s32[2,4,1]{1,2,0:T(1,128)S(1)}, s32[2,4,1]{1,2,0:T(1,128)S(1)}, u32[]{:S(2)}, u32[]{:S(2)}) collective-permute-start(s32[2,4,1]{1,2,0:T(1,128)S(1)} %collective-permute-done.4), channel_id=1, source_target_pairs={{0,1},{1,2},{2,3},{3,4},{4,5},{5,6},{6,7},{7,0},{8,9},{9,10},{10,1... | collective-permute-start | bytes 104 | tf_op jit(solution)/shard_map/ppermute | solution.py:10
  99.1 5.7 %collective-permute-start.6 = (s32[2,4,1]{1,2,0:T(1,128)S(1)}, s32[2,4,1]{1,2,0:T(1,128)S(1)}, u32[]{:S(2)}, u32[]{:S(2)}) collective-permute-start(s32[2,4,1]{1,2,0:T(1,128)S(1)} %collective-permute-done.5), channel_id=1, source_target_pairs={{0,1},{1,2},{2,3},{3,4},{4,5},{5,6},{6,7},{7,0},{8,9},{9,10},{10,1... | collective-permute-start | bytes 104 | tf_op jit(solution)/shard_map/ppermute | solution.py:10
  104.9 10.6 %collective-permute-start.11 = (bf16[2,4,1,128,128]{4,3,0,1,2:T(8,128)(2,1)S(1)}, bf16[2,4,1,128,128]{4,3,0,1,2:T(8,128)(2,1)S(1)}, u32[]{:S(2)}, u32[]{:S(2)}) collective-permute-start(bf16[2,4,1,128,128]{4,3,0,1,2:T(8,128)(2,1)S(1)} %collective-permute-done.10), channel_id=1, source_target_pairs={{0,1},{1,2},{2,3},{3,4},{4,5},{5,6},{6,7},{7,0},{8,9},{9,10},{10,1... | collective-permute-start | bytes 786440 | tf_op jit(solution)/shard_map/ppermute | solution.py:10
  115.5 10.9 %collective-permute-start.12 = (bf16[2,4,1,128,128]{4,3,0,1,2:T(8,128)(2,1)S(1)}, bf16[2,4,1,128,128]{4,3,0,1,2:T(8,128)(2,1)S(1)}, u32[]{:S(2)}, u32[]{:S(2)}) collective-permute-start(bf16[2,4,1,128,128]{4,3,0,1,2:T(8,128)(2,1)S(1)} %collective-permute-done.11), channel_id=1, source_target_pairs={{0,1},{1,2},{2,3},{3,4},{4,5},{5,6},{6,7},{7,0},{8,9},{9,10},{10,1... | collective-permute-start | bytes 786440 | tf_op jit(solution)/shard_map/ppermute | solution.py:10
  126.4 8.5 %collective-permute-start.13 = (bf16[2,4,1,128,128]{4,3,0,1,2:T(8,128)(2,1)S(1)}, bf16[2,4,1,128,128]{4,3,0,1,2:T(8,128)(2,1)S(1)}, u32[]{:S(2)}, u32[]{:S(2)}) collective-permute-start(bf16[2,4,1,128,128]{4,3,0,1,2:T(8,128)(2,1)S(1)} %collective-permute-done.12), channel_id=1, source_target_pairs={{0,1},{1,2},{2,3},{3,4},{4,5},{5,6},{6,7},{7,0},{8,9},{9,10},{10,1... | collective-permute-start | bytes 786440 | tf_op jit(solution)/shard_map/ppermute | solution.py:10
  135.6 151.5 %copy-start.2 = (s32[2,4,2]{1,2,0:T(2,128)S(1)}, s32[2,4,2]{1,2,0:T(2,128)}, u32[]{:S(2)}) copy-start(s32[2,4,2]{1,2,0:T(2,128)} %param.9) | copy-start | bytes 196
  270.6 112.1 %copy-start = (bf16[2,4,2,128,128]{4,3,2,1,0:T(8,128)(2,1)}, bf16[2,4,2,128,128]{4,3,2,1,0:T(8,128)(2,1)S(1)}, u32[]{:S(2)}) copy-start(bf16[2,4,2,128,128]{4,3,2,1,0:T(8,128)(2,1)S(1)} %copy.57) | copy-start | bytes 1572868
  270.6 16.6 %collective-permute-start.21 = (bf16[2,4,2,128,128]{4,3,2,1,0:T(8,128)(2,1)S(1)}, bf16[2,4,2,128,128]{4,3,2,1,0:T(8,128)(2,1)S(1)}, u32[]{:S(2)}, u32[]{:S(2)}) collective-permute-start(bf16[2,4,2,128,128]{4,3,2,1,0:T(8,128)(2,1)S(1)} %copy.57), channel_id=1, source_target_pairs={{0,1},{1,2},{2,3},{3,4},{4,5},{5,6},{6,7},{7,0},{8,9},{9,10},{10,1... | collective-permute-start | bytes 1572872 | tf_op jit(solution)/shard_map/ppermute | solution.py:10
  287.1 16.2 %collective-permute-start.22 = (bf16[2,4,2,128,128]{4,3,2,1,0:T(8,128)(2,1)S(1)}, bf16[2,4,2,128,128]{4,3,2,1,0:T(8,128)(2,1)S(1)}, u32[]{:S(2)}, u32[]{:S(2)}) collective-permute-start(bf16[2,4,2,128,128]{4,3,2,1,0:T(8,128)(2,1)S(1)} %collective-permute-done.21), channel_id=1, source_target_pairs={{0,1},{1,2},{2,3},{3,4},{4,5},{5,6},{6,7},{7,0},{8,9},{9,10},{10,1... | collective-permute-start | bytes 1572872 | tf_op jit(solution)/shard_map/ppermute | solution.py:10
  287.2 16.2 %collective-permute-start.14 = (s32[2,4,2]{1,2,0:T(2,128)S(1)}, s32[2,4,2]{1,2,0:T(2,128)S(1)}, u32[]{:S(2)}, u32[]{:S(2)}) collective-permute-start(s32[2,4,2]{1,2,0:T(2,128)S(1)} %copy-done.2), channel_id=1, source_target_pairs={{0,1},{1,2},{2,3},{3,4},{4,5},{5,6},{6,7},{7,0},{8,9},{9,10},{10,1... | collective-permute-start | bytes 200 | tf_op jit(solution)/shard_map/ppermute | solution.py:10
  303.3 19.7 %collective-permute-start.23 = (bf16[2,4,2,128,128]{4,3,2,1,0:T(8,128)(2,1)S(1)}, bf16[2,4,2,128,128]{4,3,2,1,0:T(8,128)(2,1)S(1)}, u32[]{:S(2)}, u32[]{:S(2)}) collective-permute-start(bf16[2,4,2,128,128]{4,3,2,1,0:T(8,128)(2,1)S(1)} %collective-permute-done.22), channel_id=1, source_target_pairs={{0,1},{1,2},{2,3},{3,4},{4,5},{5,6},{6,7},{7,0},{8,9},{9,10},{10,1... | collective-permute-start | bytes 1572872 | tf_op jit(solution)/shard_map/ppermute | solution.py:10
  303.4 13.9 %collective-permute-start.15 = (s32[2,4,2]{1,2,0:T(2,128)S(1)}, s32[2,4,2]{1,2,0:T(2,128)S(1)}, u32[]{:S(2)}, u32[]{:S(2)}) collective-permute-start(s32[2,4,2]{1,2,0:T(2,128)S(1)} %collective-permute-done.14), channel_id=1, source_target_pairs={{0,1},{1,2},{2,3},{3,4},{4,5},{5,6},{6,7},{7,0},{8,9},{9,10},{10,1... | collective-permute-start | bytes 200 | tf_op jit(solution)/shard_map/ppermute | solution.py:10
  317.3 5.7 %collective-permute-start.16 = (s32[2,4,2]{1,2,0:T(2,128)S(1)}, s32[2,4,2]{1,2,0:T(2,128)S(1)}, u32[]{:S(2)}, u32[]{:S(2)}) collective-permute-start(s32[2,4,2]{1,2,0:T(2,128)S(1)} %collective-permute-done.15), channel_id=1, source_target_pairs={{0,1},{1,2},{2,3},{3,4},{4,5},{5,6},{6,7},{7,0},{8,9},{9,10},{10,1... | collective-permute-start | bytes 200 | tf_op jit(solution)/shard_map/ppermute | solution.py:10
  323.0 5.7 %collective-permute-start.17 = (s32[2,4,2]{1,2,0:T(2,128)S(1)}, s32[2,4,2]{1,2,0:T(2,128)S(1)}, u32[]{:S(2)}, u32[]{:S(2)}) collective-permute-start(s32[2,4,2]{1,2,0:T(2,128)S(1)} %collective-permute-done.16), channel_id=1, source_target_pairs={{0,1},{1,2},{2,3},{3,4},{4,5},{5,6},{6,7},{7,0},{8,9},{9,10},{10,1... | collective-permute-start | bytes 200 | tf_op jit(solution)/shard_map/ppermute | solution.py:10
  323.0 21.8 %collective-permute-start.24 = (bf16[2,4,2,128,128]{4,3,2,1,0:T(8,128)(2,1)S(1)}, bf16[2,4,2,128,128]{4,3,2,1,0:T(8,128)(2,1)}, u32[]{:S(2)}, u32[]{:S(2)}) collective-permute-start(bf16[2,4,2,128,128]{4,3,2,1,0:T(8,128)(2,1)S(1)} %collective-permute-done.23), channel_id=1, source_target_pairs={{0,1},{1,2},{2,3},{3,4},{4,5},{5,6},{6,7},{7,0},{8,9},{9,10},{10,1... | collective-permute-start | bytes 1572872 | tf_op jit(solution)/shard_map/ppermute | solution.py:10
  328.7 10.4 %collective-permute-start.18 = (s32[2,4,2]{1,2,0:T(2,128)S(1)}, s32[2,4,2]{1,2,0:T(2,128)S(1)}, u32[]{:S(2)}, u32[]{:S(2)}) collective-permute-start(s32[2,4,2]{1,2,0:T(2,128)S(1)} %collective-permute-done.17), channel_id=1, source_target_pairs={{0,1},{1,2},{2,3},{3,4},{4,5},{5,6},{6,7},{7,0},{8,9},{9,10},{10,1... | collective-permute-start | bytes 200 | tf_op jit(solution)/shard_map/ppermute | solution.py:10
  339.1 5.7 %collective-permute-start.19 = (s32[2,4,2]{1,2,0:T(2,128)S(1)}, s32[2,4,2]{1,2,0:T(2,128)S(1)}, u32[]{:S(2)}, u32[]{:S(2)}) collective-permute-start(s32[2,4,2]{1,2,0:T(2,128)S(1)} %collective-permute-done.18), channel_id=1, source_target_pairs={{0,1},{1,2},{2,3},{3,4},{4,5},{5,6},{6,7},{7,0},{8,9},{9,10},{10,1... | collective-permute-start | bytes 200 | tf_op jit(solution)/shard_map/ppermute | solution.py:10
  344.8 5.7 %collective-permute-start.20 = (s32[2,4,2]{1,2,0:T(2,128)S(1)}, s32[2,4,2]{1,2,0:T(2,128)S(1)}, u32[]{:S(2)}, u32[]{:S(2)}) collective-permute-start(s32[2,4,2]{1,2,0:T(2,128)S(1)} %collective-permute-done.19), channel_id=1, source_target_pairs={{0,1},{1,2},{2,3},{3,4},{4,5},{5,6},{6,7},{7,0},{8,9},{9,10},{10,1... | collective-permute-start | bytes 200 | tf_op jit(solution)/shard_map/ppermute | solution.py:10
  344.8 13.0 %collective-permute-start.25 = (bf16[2,4,2,128,128]{4,3,2,1,0:T(8,128)(2,1)}, bf16[2,4,2,128,128]{4,3,2,1,0:T(8,128)(2,1)}, u32[]{:S(2)}, u32[]{:S(2)}) collective-permute-start(bf16[2,4,2,128,128]{4,3,2,1,0:T(8,128)(2,1)} %collective-permute-done.24), channel_id=1, source_target_pairs={{0,1},{1,2},{2,3},{3,4},{4,5},{5,6},{6,7},{7,0},{8,9},{9,10},{10,1... | collective-permute-start | bytes 1572872 | tf_op jit(solution)/shard_map/ppermute | solution.py:10
  357.8 13.5 %collective-permute-start.26 = (bf16[2,4,2,128,128]{4,3,2,1,0:T(8,128)(2,1)}, bf16[2,4,2,128,128]{4,3,2,1,0:T(8,128)(2,1)S(1)}, u32[]{:S(2)}, u32[]{:S(2)}) collective-permute-start(bf16[2,4,2,128,128]{4,3,2,1,0:T(8,128)(2,1)} %collective-permute-done.25), channel_id=1, source_target_pairs={{0,1},{1,2},{2,3},{3,4},{4,5},{5,6},{6,7},{7,0},{8,9},{9,10},{10,1... | collective-permute-start | bytes 1572872 | tf_op jit(solution)/shard_map/ppermute | solution.py:10
  371.3 11.3 %collective-permute-start.27 = (bf16[2,4,2,128,128]{4,3,2,1,0:T(8,128)(2,1)S(1)}, bf16[2,4,2,128,128]{4,3,2,1,0:T(8,128)(2,1)S(1)}, u32[]{:S(2)}, u32[]{:S(2)}) collective-permute-start(bf16[2,4,2,128,128]{4,3,2,1,0:T(8,128)(2,1)S(1)} %collective-permute-done.26), channel_id=1, source_target_pairs={{0,1},{1,2},{2,3},{3,4},{4,5},{5,6},{6,7},{7,0},{8,9},{9,10},{10,1... | collective-permute-start | bytes 1572872 | tf_op jit(solution)/shard_map/ppermute | solution.py:10
  382.7 2.0 copy-start.1
Sparse Core Ops, SparseCore 0:
  10.7 109.4 all-gather.1
where the time goes:
time: 554 us; the launch traced here: 550 us
  waiting for transfers between devices  184 us (33%)
  local copies, waits for them, and re-layouts  176 us (32%)
  matrix products  102 us (18%)
  blocking collectives  37.1 us (7%)
  other arithmetic  21.8 us (4%)
  between operations  14.2 us (3%)
  loops' own time  7.37 us (1%)
  starting transfers between devices  6.95 us (1%)
    ppermute x28, waiting for transfers between devices, shifted(): return lax.ppermute(value, axis, pairs)  183 us
    dot_general x64, matrix products, one_slab(): jnp.einsum('iamn,iaqtnk->iqtmk', a_tiles, selected, preferred_element_typ...  102 us
    dynamic_slice x64, local copies, waits for them, and re-layouts, one_slab(): lax.dynamic_slice_in_dim(piece_tiles, step * slab_rows, slab_rows, 0)  62.1 us
    gather x64, local copies, waits for them, and re-layouts, one_slab(): b_rows = jnp.take(b_tiles, a_cols, axis=0)  39.9 us
    all_gather x1, blocking collectives, shards(): lax.all_gather(x_cols, 'row', axis=0, tiled=True)  37.1 us
    gather x64, local copies, waits for them, and re-layouts, one_slab(): b_ids = jnp.take(b_cols, a_cols, axis=0)  35.8 us
    another operation x64, local copies, waits for them, and re-layouts  16.9 us
    unnamed x38, local copies, waits for them, and re-layouts  13.5 us
  transfers between devices with their start and end apart: 29, of which 21 were waited for; matrix products, arithmetic and copies ran while one was open for 2% of the time, Pallas kernels for 0%

commit v1 on v0

v1 whole, which is shorter than its diff:
```python
import functools

import jax
import jax.numpy as jnp
from jax import lax
from jax.experimental import pallas as pl
from jax.experimental.pallas import tpu as pltpu
from jax.sharding import PartitionSpec as P

T = 128
HEAD = 16
ROWS = HEAD + 8 * T
NP = 4
BF = jnp.bfloat16
F32 = jnp.float32


def span(panel):
    return (0, HEAD + 2 * T) if panel == 0 else (HEAD + 2 * T * panel, 2 * T)


def half_span(panel, which):
    first, size = span(panel)
    cut = size - T
    return (first, cut) if which == 0 else (first + cut, T)


A_HALF = ((0, HEAD + 4 * T), (HEAD + 4 * T, 4 * T))


def kernel(
    x_hbm, xc, kc, sq_hbm, pu_hbm,
    b_raw, bd, a_raw, a_dense, s_buf, acc, part, sq_v, pu_v,
    load_sem, xh_s, xh_r, z_s, z_r, core_s, core_r,
    a_s, ax_r, ay_r, s_s, sx_r, sy_r, out_sem,
):
    row = lax.axis_index("row")
    me_c = lax.axis_index("col")
    xhi, z, core = row // 16, (row // 2) % 8, row % 2
    y, xlo = me_c // 2, me_c % 2

    def row_of(a, b, c):
        return (a * 8 + b) * 2 + c

    z_peer = (row_of(xhi, (z + 1) % 8, core), row_of(xhi, (z + 7) % 8, core))
    xh_peer = row_of(1 - xhi, z, core)
    core_peer = row_of(xhi, z, 1 - core)
    y_peer = (((y + 1) % 4) * 2 + xlo, ((y + 3) % 4) * 2 + xlo)
    xl_peer = y * 2 + 1 - xlo

    own_b = b_raw.at[core, z, xhi]
    own_a = a_raw.at[me_c]
    loads = []
    for panel in range(NP):
        for i in range(2):
            rows = pl.ds(HEAD + 2 * T * panel + T * i, T)
            loads.append(pltpu.make_async_copy(x_hbm.at[i, panel, 0], own_b.at[rows], load_sem.at[0, panel, i]))
            loads.append(pltpu.make_async_copy(x_hbm.at[i, panel, 0], own_a.at[rows], load_sem.at[1, panel, i]))
    for copy in loads:
        copy.start()

    line = lax.broadcasted_iota(jnp.int32, (HEAD, T), 0)
    flags = jnp.zeros((HEAD, T), jnp.int32)
    for i in range(2):
        for panel in range(NP):
            flags = jnp.where(line == i * NP + panel, xc[i, panel, 0], flags)
    flags = flags.astype(F32).astype(BF)
    own_b[0:HEAD, :] = flags
    own_a[0:HEAD, :] = flags

    barrier = pltpu.get_barrier_semaphore()
    for peer in (z_peer[0], z_peer[1], xh_peer, core_peer):
        pl.semaphore_signal(barrier, inc=1, device_id={"row": peer}, device_id_type=pl.DeviceIdType.MESH)
    for peer in (y_peer[0], y_peer[1], xl_peer):
        pl.semaphore_signal(barrier, inc=1, device_id={"col": peer}, device_id_type=pl.DeviceIdType.MESH)
    pl.semaphore_wait(barrier, 7)
    for copy in loads:
        copy.wait()

    def remote(ref, send, recv, target):
        return pltpu.make_async_remote_copy(
            src_ref=ref, dst_ref=ref, send_sem=send, recv_sem=recv,
            device_id=target, device_id_type=pl.DeviceIdType.MESH,
        )

    def xh_copy(panel, plane):
        ref = b_raw.at[core, z, plane, pl.ds(*span(panel))]
        return remote(ref, xh_s, xh_r.at[panel], {"row": xh_peer})

    def z_copy(way, panel, hop, e, source):
        plane = xhi if e == 0 else 1 - xhi
        where = span(panel) if hop < 4 else half_span(panel, way)
        ref = b_raw.at[core, source, plane, pl.ds(*where)]
        return remote(ref, z_s.at[panel], z_r.at[way, panel, hop - 1, e], {"row": z_peer[way]})

    def behind(way, count):
        return (z + (8 - count if way == 0 else count)) % 8

    def z_send(way, panel, hop, e):
        z_copy(way, panel, hop, e, behind(way, hop - 1)).start()

    def z_wait(way, panel, hop, e):
        z_copy(way, panel, hop, e, behind(way, hop)).wait_recv()

    def core_send(panel, source, e, where):
        plane = xhi if e == 0 else 1 - xhi
        ref = b_raw.at[core, source, plane, pl.ds(*where)]
        remote(ref, core_s.at[panel], core_r.at[panel], {"row": core_peer}).start()

    def row_copy(buf, owner, where, send, recv, target):
        return remote(buf.at[owner, pl.ds(*where)], send, recv, {"col": target})

    class Gather:
        def __init__(self, buf, halves, send, x_recv, y_recv):
            self.buf, self.halves, self.send = buf, halves, send
            self.x_recv, self.y_recv = x_recv, y_recv
            self.total = halves[0][1] + halves[1][1]

        def owner(self, e, way, count):
            side = (y + (4 - count if way == 0 else count)) % 4
            return side * 2 + (xlo if e == 0 else 1 - xlo)

        def x_copy(self, owner):
            return row_copy(self.buf, owner, (0, self.total), self.send, self.x_recv, xl_peer)

        def y_copy(self, e, way, hop, which, owner):
            slot = which if hop == 1 else 2
            return row_copy(self.buf, owner, self.halves[which], self.send, self.y_recv.at[e, way, slot], y_peer[way])

        def send_y(self, e):
            for order in range(2):
                for way in range(2):
                    which = order if way == 0 else 1 - order
                    self.y_copy(e, way, 1, which, self.owner(e, way, 0)).start()

        def send_x(self):
            self.x_copy(me_c).start()

        def pass_x(self):
            self.x_copy(xl_peer).wait_recv()
            self.send_y(1)

        def pass_y(self, e):
            for way in range(2):
                self.y_copy(e, way, 1, way, self.owner(e, way, 1)).wait_recv()
                self.y_copy(e, way, 2, way, self.owner(e, way, 1)).start()

        def finish(self, e):
            for way in range(2):
                self.y_copy(e, way, 1, 1 - way, self.owner(e, way, 1)).wait_recv()
            for way in range(2):
                self.y_copy(e, way, 2, way, self.owner(e, way, 2)).wait_recv()

        def drain(self):
            done = self.buf.at[0:7]
            pltpu.make_async_copy(done, done, self.send).wait()

    a_g = Gather(a_raw, A_HALF, a_s, ax_r, ay_r)
    s_g = [
        Gather(s_buf.at[panel], ((0, T), (T, T)), s_s.at[panel], sx_r.at[panel], sy_r.at[panel])
        for panel in range(NP)
    ]

    def mask_of(flag_rows, index):
        wide = jnp.broadcast_to(flag_rows[index : index + 1, :], (HEAD, T)).astype(BF)
        return jnp.concatenate([wide] * (T // HEAD), axis=0)

    def split(tile, mask):
        return tile * (jnp.ones_like(mask) - mask), tile * mask

    def dense_b(panel):
        def body(r, _):
            block = b_raw.at[r % 2, (r // 2) % 8, r // 16]
            flag_rows = block[0:HEAD, :].astype(F32)
            base = pl.multiple_of(((r % 4) * 8 + r // 4) * 2 * T, 2 * T)
            for i in range(2):
                tile = block[HEAD + 2 * T * panel + T * i : HEAD + 2 * T * panel + T * (i + 1), :]
                left, right = split(tile, mask_of(flag_rows, i * NP + panel))
                rows = pl.ds(base + T * i, T)
                bd[panel, rows, 0:T] = left
                bd[panel, rows, T : 2 * T] = right
            return 0

        lax.fori_loop(0, 32, body, 0)

    def dense_a():
        for owner in range(8):
            def body(owner=owner):
                block = a_raw.at[owner]
                flag_rows = block[0:HEAD, :].astype(F32)
                for panel in range(NP):
                    for i in range(2):
                        tile = block[HEAD + 2 * T * panel + T * i : HEAD + 2 * T * panel + T * (i + 1), :]
                        left, right = split(tile, mask_of(flag_rows, i * NP + panel))
                        lanes = owner * 2 * T
                        a_dense[panel, T * i : T * (i + 1), lanes : lanes + T] = left
                        a_dense[panel, T * i : T * (i + 1), lanes + T : lanes + 2 * T] = right

            body()

    def choose(i, panel, t, left, right):
        pick = jnp.full((T, T), kc[i, panel, t], jnp.int32)
        return jnp.where(pick == 0, left, right)

    def square(panel):
        part[...] = jnp.zeros_like(part)

        def body(group, _):
            rows = pl.ds(pl.multiple_of(group * 2048, 2048), 2048)
            part[...] += jnp.dot(a_dense[group], bd[panel, rows, :], preferred_element_type=F32)
            return 0

        lax.fori_loop(0, NP, body, 0)
        s_buf[panel, me_c] = part[...].astype(BF)

    def square_out(panel):
        for i in range(2):
            value = s_buf[panel, me_c, T * i : T * (i + 1), :].astype(F32)
            for t in range(2):
                sq_v[i, panel, t] = choose(i, panel, t, value[:, 0:T], value[:, T:]).astype(BF)
        pltpu.make_async_copy(sq_v.at[:, panel], sq_hbm.at[:, panel], out_sem.at[0, panel]).start()

    def cube(group, low, high):
        lhs = jnp.concatenate([s_buf[group, owner] for owner in range(8)], axis=1)

        def body(panel, _):
            got = jnp.dot(lhs, bd[panel, group * 2048 : (group + 1) * 2048, :], preferred_element_type=F32)
            if group == 0:
                acc[panel] = got
            else:
                acc[panel] += got
            return 0

        lax.fori_loop(low, high, body, 0)

    def result(panel):
        for i in range(2):
            own = s_buf[panel, me_c, T * i : T * (i + 1), :].astype(F32)
            value = 3.0 * own - 2.0 * acc[panel, T * i : T * (i + 1), :]
            for t in range(2):
                pu_v[i, panel, t] = choose(i, panel, t, value[:, 0:T], value[:, T:]).astype(BF)
        pltpu.make_async_copy(pu_v.at[:, panel], pu_hbm.at[:, panel], out_sem.at[1, panel]).start()

    def complete(panel):
        for e in range(2):
            for way in range(2):
                z_wait(way, panel, 4, e)
                core_send(panel, behind(way, 4), e, half_span(panel, way))
        other = b_raw.at[1 - core, :, :, pl.ds(*span(panel))]
        pltpu.make_async_copy(other, other, core_r.at[panel]).wait()
        dense_b(panel)
        square(panel)
        s_g[panel].send_y(0)
        s_g[panel].send_x()
        square_out(panel)

    def start_panel(panel):
        if panel > 0:
            for way in range(2):
                z_send(way, panel, 1, 0)
            core_send(panel, z, 0, span(panel))
        xh_copy(panel, 1 - xhi).wait_recv()
        for way in range(2):
            z_send(way, panel, 1, 1)
        core_send(panel, z, 1, span(panel))

    def advance(panel, hop):
        for e in range(2):
            for way in range(2):
                z_wait(way, panel, hop - 1, e)
                z_send(way, panel, hop, e)
                core_send(panel, behind(way, hop - 1), e, span(panel))

    xh_copy(0, xhi).start()
    for way in range(2):
        z_send(way, 0, 1, 0)
    a_g.send_x()
    a_g.send_y(0)
    for panel in range(1, NP):
        xh_copy(panel, xhi).start()
    core_send(0, z, 0, span(0))

    for turn in range(14):
        for panel in range(NP):
            hop = turn - 2 * panel + 1
            if hop == 1:
                start_panel(panel)
            elif 2 <= hop <= 4:
                advance(panel, hop)
        if turn == 1:
            a_g.pass_x()
        if turn == 2:
            a_g.pass_y(0)
        if turn == 3:
            a_g.pass_y(1)
        if turn == 4:
            a_g.finish(0)
            a_g.finish(1)
            dense_a()
        for panel in range(NP):
            ready = 2 * panel + 4
            if turn == ready + 1:
                s_g[panel].pass_x()
            if turn == ready + 2:
                s_g[panel].pass_y(0)
                s_g[panel].pass_y(1)
        for panel in range(NP):
            ready = 2 * panel + 4
            if turn == ready:
                complete(panel)
                for group in range(panel - 1):
                    cube(group, panel, panel + 1)
            if turn == ready + 3:
                s_g[panel].finish(0)
                s_g[panel].finish(1)
                cube(panel, 0, min(panel + 2, NP))
    for panel in range(NP):
        result(panel)

    for panel in range(NP):
        sent = b_raw.at[0, 0:7, :, pl.ds(*span(panel))]
        pltpu.make_async_copy(sent, sent, z_s.at[panel]).wait()
        sent = b_raw.at[0, :, :, pl.ds(*span(panel))]
        pltpu.make_async_copy(sent, sent, core_s.at[panel]).wait()
        s_g[panel].drain()
    a_g.drain()
    sent = b_raw.at[0, 0, 0]
    pltpu.make_async_copy(sent, sent, xh_s).wait()
    for panel in range(NP):
        pltpu.make_async_copy(sq_v.at[:, panel], sq_hbm.at[:, panel], out_sem.at[0, panel]).wait()
        pltpu.make_async_copy(pu_v.at[:, panel], pu_hbm.at[:, panel], out_sem.at[1, panel]).wait()


def shards(x_tiles, x_cols, keep_cols):
    dma = pltpu.SemaphoreType.DMA
    out = jax.ShapeDtypeStruct((2, NP, 2, T, T), BF)
    return tuple(
        pl.pallas_call(
            kernel,
            out_shape=(out, out),
            in_specs=[
                pl.BlockSpec(memory_space=pl.ANY),
                pl.BlockSpec(memory_space=pltpu.SMEM),
                pl.BlockSpec(memory_space=pltpu.SMEM),
            ],
            out_specs=(pl.BlockSpec(memory_space=pl.ANY), pl.BlockSpec(memory_space=pl.ANY)),
            scratch_shapes=[
                pltpu.VMEM((2, 8, 2, ROWS, T), BF),
                pltpu.VMEM((NP, 64 * T, 2 * T), BF),
                pltpu.VMEM((8, ROWS, T), BF),
                pltpu.VMEM((NP, 2 * T, 16 * T), BF),
                pltpu.VMEM((NP, 8, 2 * T, 2 * T), BF),
                pltpu.VMEM((NP, 2 * T, 2 * T), F32),
                pltpu.VMEM((2 * T, 2 * T), F32),
                pltpu.VMEM((2, NP, 2, T, T), BF),
                pltpu.VMEM((2, NP, 2, T, T), BF),
                dma((2, NP, 2)),
                dma,
                dma((NP,)),
                dma((NP,)),
                dma((2, NP, 4, 2)),
                dma((NP,)),
                dma((NP,)),
                dma,
                dma,
                dma((2, 2, 3)),
                dma((NP,)),
                dma((NP,)),
                dma((NP, 2, 2, 3)),
                dma((2, NP)),
            ],
            compiler_params=pltpu.CompilerParams(
                collective_id=0, has_side_effects=True, vmem_limit_bytes=60 * 1024 * 1024
            ),
        )(x_tiles, x_cols, keep_cols)
    )


def solution(mesh):
    in_specs = (P("row", "col", None, None, None), P("row", "col", None), P("row", "col", None))
    out_specs = (P("row", "col", None, None, None), P("row", "col", None, None, None))
    return jax.shard_map(shards, mesh=mesh, in_specs=in_specs, out_specs=out_specs, check_vma=False)
```

time: 554 us -> 100 us (0.18)
  the two profiles are of different devices: /device:TPU:68 before, /device:TPU:1 now
where the time goes in v1:
time: 100 us; the launch traced here: 99.8 us
  Pallas kernels  94.4 us (94%)
  local copies, waits for them, and re-layouts  4.79 us (5%)
    pallas_call x1, Pallas kernels, shards(): pl.pallas_call(kernel, out_shape=(out, out), in_specs=[pl.BlockSpec(memor...  94.4 us
    unnamed x8, local copies, waits for them, and re-layouts  4.79 us

profile of v1, /device:TPU:1, one launch (start us, length us, event | category | flops | bytes accessed | tf_op | source)
XLA Modules:
  0.0 99.8 jit_solution(6488118607668597789)
XLA Ops:
  0.6 0.0 copy-start.1
  0.6 1.4 %copy.5.xc = s32[2,4,1]{2,1,0:T(4,128)} copy(s32[2,4,1]{1,2,0:T(1,128)} %param.4) | data formatting | bytes 64 | tf_op args[1]
  2.0 0.0 copy-done.1
  2.0 0.7 copy.6.kc
  2.7 94.4 %shard_map.50 = (bf16[2,4,2,128,128]{4,3,2,1,0:T(8,128)(2,1)}, bf16[2,4,2,128,128]{4,3,2,1,0:T(8,128)(2,1)}) custom-call(bf16[2,4,1,128,128]{4,3,2,1,0:T(8,128)(2,1)} %x_hbm.1, s32[2,4,1]{2,1,0:T(4,128)} %copy.5.xc, s32[2,4,2]{2,1,0:T(4,128)} %copy.6.kc), custom_call_target="tpu_custom_call" | custom-call | tf_op jit(solution)/shard_map/pallas_call | solution.py:338
  97.1 0.0 copy-start
  97.1 1.9 %copy.9 = bf16[2,4,2,128,128]{4,3,2,1,0:T(8,128)(2,1)} copy(bf16[2,4,2,128,128]{4,3,2,1,0:T(8,128)(2,1)} %get-tuple-element.4) | data formatting | bytes 1048576
  99.0 0.0 copy-done
  99.0 0.8 copy.10
Async XLA Ops:
  0.6 1.4 %copy-start.1 = (s32[2,4,2]{1,2,0:T(2,128)S(1)}, s32[2,4,2]{1,2,0:T(2,128)}, u32[]{:S(2)}) copy-start(s32[2,4,2]{1,2,0:T(2,128)} %param.5) | copy-start | bytes 196
  97.1 2.0 %copy-start = (bf16[2,4,2,128,128]{4,3,2,1,0:T(8,128)(2,1)S(1)}, bf16[2,4,2,128,128]{4,3,2,1,0:T(8,128)(2,1)}, u32[]{:S(2)}) copy-start(bf16[2,4,2,128,128]{4,3,2,1,0:T(8,128)(2,1)} %get-tuple-element.5) | copy-start | bytes 1572868

commit v2 on v1

--- a/solution.py
+++ b/solution.py
@@ -233,6 +233,18 @@
 
         lax.fori_loop(low, high, body, 0)
 
+    def half_cube(group, e):
+        owners = [side * 2 + (xlo if e == 0 else 1 - xlo) for side in range(4)]
+        lhs = jnp.concatenate([s_buf[group, owner] for owner in owners], axis=1)
+        rows = [pl.ds(pl.multiple_of(group * 2048 + owner * 256, 256), 256) for owner in owners]
+
+        def body(panel, _):
+            rhs = jnp.concatenate([bd[panel, where, :] for where in rows], axis=0)
+            acc[panel] += jnp.dot(lhs, rhs, preferred_element_type=F32)
+            return 0
+
+        lax.fori_loop(0, NP, body, 0)
+
     def result(panel):
         for i in range(2):
             own = s_buf[panel, me_c, T * i : T * (i + 1), :].astype(F32)
@@ -280,9 +292,9 @@
         xh_copy(panel, xhi).start()
     core_send(0, z, 0, span(0))
 
-    for turn in range(14):
+    for turn in range(11):
         for panel in range(NP):
-            hop = turn - 2 * panel + 1
+            hop = turn - panel + 1
             if hop == 1:
                 start_panel(panel)
             elif 2 <= hop <= 4:
@@ -298,22 +310,27 @@
             a_g.finish(1)
             dense_a()
         for panel in range(NP):
-            ready = 2 * panel + 4
+            ready = panel + 4
             if turn == ready + 1:
                 s_g[panel].pass_x()
             if turn == ready + 2:
                 s_g[panel].pass_y(0)
                 s_g[panel].pass_y(1)
         for panel in range(NP):
-            ready = 2 * panel + 4
+            ready = panel + 4
             if turn == ready:
                 complete(panel)
-                for group in range(panel - 1):
+                for group in range(panel - 2):
                     cube(group, panel, panel + 1)
             if turn == ready + 3:
                 s_g[panel].finish(0)
+                if panel == NP - 1:
+                    half_cube(panel, 0)
+                    s_g[panel].finish(1)
+                    half_cube(panel, 1)
+                    continue
                 s_g[panel].finish(1)
-                cube(panel, 0, min(panel + 2, NP))
+                cube(panel, 0, min(panel + 3, NP))
     for panel in range(NP):
         result(panel)
 

time: 100 us -> 98.6 us (0.986)
  Pallas kernels: 94.4 us -> 92.7 us
    pallas_call x1, Pallas kernels: 94.4 us -> 92.7 us  [shards(): pl.pallas_call(kernel, out_shape=(out, out), in_specs=[pl.BlockSpec(memor...]
where the time goes in v2:
time: 98.6 us; the launch traced here: 98.2 us
  Pallas kernels  92.7 us (94%)
  local copies, waits for them, and re-layouts  4.79 us (5%)
    pallas_call x1, Pallas kernels, shards(): pl.pallas_call(kernel, out_shape=(out, out), in_specs=[pl.BlockSpec(memor...  92.7 us
    unnamed x8, local copies, waits for them, and re-layouts  4.79 us

profile of v2, /device:TPU:1, one launch (start us, length us, event | category | flops | bytes accessed | tf_op | source)
XLA Modules:
  0.0 98.2 jit_solution(11494303311665859797)
XLA Ops:
  0.6 0.0 copy-start.1
  0.6 1.4 %copy.5.xc = s32[2,4,1]{2,1,0:T(4,128)} copy(s32[2,4,1]{1,2,0:T(1,128)} %param.4) | data formatting | bytes 64 | tf_op args[1]
  2.0 0.0 copy-done.1
  2.0 0.7 copy.6.kc
  2.7 92.7 %shard_map.50 = (bf16[2,4,2,128,128]{4,3,2,1,0:T(8,128)(2,1)}, bf16[2,4,2,128,128]{4,3,2,1,0:T(8,128)(2,1)}) custom-call(bf16[2,4,1,128,128]{4,3,2,1,0:T(8,128)(2,1)} %x_hbm.1, s32[2,4,1]{2,1,0:T(4,128)} %copy.5.xc, s32[2,4,2]{2,1,0:T(4,128)} %copy.6.kc), custom_call_target="tpu_custom_call" | custom-call | tf_op jit(solution)/shard_map/pallas_call | solution.py:355
  95.4 0.0 copy-start
  95.5 1.9 %copy.9 = bf16[2,4,2,128,128]{4,3,2,1,0:T(8,128)(2,1)} copy(bf16[2,4,2,128,128]{4,3,2,1,0:T(8,128)(2,1)} %get-tuple-element.4) | data formatting | bytes 1048576
  97.4 0.0 copy-done
  97.4 0.8 copy.10
Async XLA Ops:
  0.6 1.4 %copy-start.1 = (s32[2,4,2]{1,2,0:T(2,128)S(1)}, s32[2,4,2]{1,2,0:T(2,128)}, u32[]{:S(2)}) copy-start(s32[2,4,2]{1,2,0:T(2,128)} %param.5) | copy-start | bytes 196
  95.4 2.0 %copy-start = (bf16[2,4,2,128,128]{4,3,2,1,0:T(8,128)(2,1)S(1)}, bf16[2,4,2,128,128]{4,3,2,1,0:T(8,128)(2,1)}, u32[]{:S(2)}) copy-start(bf16[2,4,2,128,128]{4,3,2,1,0:T(8,128)(2,1)} %get-tuple-element.5) | copy-start | bytes 1572868
